TPU v7x, 32 devices: a whole 2x2x4 slice. The times are simulated.
32 devices in a mesh: gx: 2 (over x), gz: 4 (over y, core), ta: 4 (over z).
Axes of the slice: x: 2, y: 2, z: 4, core: 2. Of those that a mesh axis runs over, the one named last changes fastest.
Arguments:
- velocity: bfloat16 [3, 32, 64, 4096], P(None, 'ta', 'gx', 'gz'), may hold values from -6 to 6
- offsets: int32 [7], replicated, may hold values from 0 to 16, as said below
- owner: int32 [7], replicated, may hold values from 0 to 7, as said below
Outputs:
- cross_spectra: float32 [4, 2, 7, 64, 4096], P(None, None, None, 'gx', ('gz', 'ta'))
Inputs may be any that keep to these rules, and one draw needn't show every extreme that they name: `offsets`: each segment of 16 snapshots lies inside the window. owner o names the block of streamwise index o // 4 and spanwise index o mod 4.
All inputs are finite; a program needn't handle non-finite values.
Results may differ from a plain program's by a relative error of at most 0.0062.
Values may be sent and summed in bfloat16 or wider, within the bound.
No kernel may reach another device: no remote copies, remote signals or barrier semaphores. Data moves between devices by JAX's collectives and lax.ppermute only.
A program may use at most 64 MiB of HBM per device.

v0:
```python
import math
import jax
import jax.numpy as jnp
from jax import lax
from jax.sharding import PartitionSpec as P

SEG = 16
NSEG = 7
F = 7


def from_root(shard, axis, root):
    mine = lax.axis_index(axis) == root
    return lax.psum(jnp.where(mine, shard, jnp.zeros_like(shard)), axis)


def padded_2(shard, sides, width):
    for axis, dim in sides:
        devices, length = (lax.axis_size(axis), shard.shape[dim])
        up = [(i, (i + 1) % devices) for i in range(devices)]
        down = [(j, i) for i, j in up]
        last = lax.slice_in_dim(shard, length - width, length, axis=dim)
        first = lax.slice_in_dim(shard, 0, width, axis=dim)
        before = lax.ppermute(last, axis, up)
        after = lax.ppermute(first, axis, down)
        shard = jnp.concatenate([before, shard, after], axis=dim)
    return shard


def dft_table(offsets, step_count_total):
    sample_times = jnp.arange(step_count_total, dtype=jnp.int32)
    temporal_delay = sample_times[None, :] - offsets[:, None]
    inside = (temporal_delay >= 0) & (temporal_delay < SEG)
    window = 0.5 - 0.5 * jnp.cos(2.0 * math.pi / SEG * temporal_delay.astype(jnp.float32))
    frequency = jnp.arange(1, F + 1, dtype=jnp.int32)
    turns = frequency[None, :, None] * temporal_delay[:, None, :] % SEG
    phase_angle = 2.0 * math.pi / SEG * turns.astype(jnp.float32)
    weight = jnp.where(inside, window, jnp.float32(0.0))[:, None, :]
    rows = jnp.stack([weight * jnp.cos(phase_angle), -weight * jnp.sin(phase_angle)], axis=1)
    return rows.reshape(offsets.shape[0] * 2 * F, step_count_total).astype(jnp.bfloat16)


def fourth_order(padded, which_axis, length_cells):

    def shifted(first):
        return lax.slice_in_dim(padded, first, first + length_cells, axis=which_axis)

    return (8.0 * (shifted(3) - shifted(1)) - (shifted(4) - shifted(0))) / 12.0


def spread_series(block_data, root_index):
    return from_root(block_data, ("gx", "gz"), root_index)


def shards(velocity, offsets, owner):
    block_rows = velocity.shape[2]
    block_cols = velocity.shape[3]
    stream_span = jnp.stack([velocity[0], velocity[2]])
    padded = padded_2(stream_span, (("gx", 2), ("gz", 3)), 2).astype(jnp.float32)
    streamwise = padded[0, :, 2 : 2 + block_rows, :]
    spanwise = padded[1, :, :, 2 : 2 + block_cols]
    vorticity = (
        fourth_order(streamwise, 2, block_cols) - fourth_order(spanwise, 1, block_rows)
    ).astype(jnp.bfloat16)
    fields = jnp.concatenate([velocity, vorticity[None]], axis=0)
    step_count_total = velocity.shape[1] * lax.axis_size("ta")
    segment_rows = dft_table(offsets, step_count_total)
    series = lax.all_to_all(fields, "ta", split_axis=3, concat_axis=1, tiled=True)
    flat_series = series.reshape(series.shape[0], series.shape[1], -1)
    power_spectra = jnp.einsum(
        "rt,qtn->qrn", segment_rows, flat_series, preferred_element_type=jnp.float32
    )
    flat_series, power_spectra = (flat_series, power_spectra)
    quantities = flat_series.shape[0]
    cells_here = flat_series.shape[2]
    slab_cols = cells_here // block_rows
    window_rows = dft_table(jnp.zeros((1,), jnp.int32), SEG)
    cospectrum = jnp.zeros((quantities, F, cells_here), jnp.float32)
    quadrature_spectrum = jnp.zeros((quantities, F, cells_here), jnp.float32)
    for segment in range(NSEG):
        local_spec = power_spectra[:, segment * 2 * F : (segment + 1) * 2 * F, :]
        window_piece = lax.dynamic_slice_in_dim(flat_series, offsets[segment], SEG, 1)
        arrived = spread_series(window_piece, owner[segment])
        remote = jnp.einsum("rt,qtn->qrn", window_rows, arrived, preferred_element_type=jnp.float32)
        remote_cos = remote[:, :F]
        remote_sin = remote[:, F:]
        cosine_part_here = local_spec[:, :F]
        local_sin = local_spec[:, F:]
        cospectrum = cospectrum + (remote_cos * cosine_part_here + remote_sin * local_sin)
        quadrature_spectrum = quadrature_spectrum + (
            remote_cos * local_sin - remote_sin * cosine_part_here
        )
    scaling = 8.0 / (3.0 * SEG * NSEG)
    result = jnp.stack([cospectrum, quadrature_spectrum], axis=1) * scaling
    return result.reshape(quantities, 2, F, block_rows, slab_cols)


def solution(mesh):
    in_specs = (P(None, "ta", "gx", "gz"), P(), P())
    out_specs = P(None, None, None, "gx", ("gz", "ta"))
    return jax.shard_map(shards, mesh=mesh, in_specs=in_specs, out_specs=out_specs, check_vma=False)
```

profile of v0, /device:TPU:0, one launch (start us, length us, event | category | flops | bytes accessed | tf_op | source)
XLA Modules:
  0.0 293.2 jit_solution(14867775583435725023)
XLA Ops:
  6.5 1.3 fusion.28
  7.8 0.1 pad_maximum_fusion.2
  8.0 0.1 fusion.30
  8.1 3.0 %collective-permute-start = (bf16[2,8,2,1024]{3,1,2,0:T(8,128)(2,1)S(1)}, bf16[2,8,2,1024]{3,1,2,0:T(8,128)(2,1)S(1)}, u32[]{:S(2)}, u32[]{:S(2)}) collective-permute-start(bf16[2,8,2,1024]{3,1,2,0:T(8,128)(2,1)S(1)} %copy.47), channel_id=1, source_target_pairs={{0,16},{16,0},{1,17},{17,1},{2,18},{18,2},{3,19},{19,3},{4,20},{20... | collective-permute-start | bytes 196616 | tf_op jit(solution)/shard_map/ppermute | solution.py:24
  11.1 0.1 collective-permute-start.1
  11.2 2.2 collective-permute-done
  13.4 0.6 constant_dynamic-update-slice_fusion.1
  14.0 1.5 collective-permute-done.1
  15.5 0.1 fusion.29
  15.6 0.1 collective-permute-start.2
  15.7 1.7 collective-permute-start.3
  17.4 6.1 %copy.34 = bf16[3,8,32,1024]{2,1,0,3:T(8,128)(2,1)} copy(bf16[3,8,32,1024]{3,2,1,0:T(8,128)(2,1)S(1)} %copy-done) | data formatting | bytes 3145728 | tf_op args[0]
  23.5 1.4 concatenate.11
  24.8 4.7 %copy.33 = bf16[2,8,36,1028]{2,1,3,0:T(8,128)(2,1)} copy(bf16[2,8,36,1028]{3,1,2,0:T(8,128)(2,1)S(1)} %concatenate.11) | data formatting | bytes 2368512 | tf_op jit(solution)/shard_map/concatenate | solution.py:26
  29.5 2.5 convert_element_type.78
  32.1 0.3 slice_bitcast_fusion.1
  32.4 1.2 slice_bitcast_fusion
  33.6 4.4 %fusion.8 = bf16[1,8,32,1024]{2,1,0,3:T(8,128)(2,1)} fusion(f32[8,36,1024]{1,0,2:T(8,128)S(1)} %slice_bitcast_fusion.1, f32[8,32,1028]{1,0,2:T(8,128)S(1)} %slice_bitcast_fusion), kind=kLoop, calls=%fused_computation.23 | loop fusion | flops 3145728 | bytes 8912896 | tf_op jit(solution)/shard_map/broadcast_in_dim | solution.py:65
  38.1 6.7 %fusion.33 = bf16[1024,4,8,32]{3,2,1,0:T(8,128)(2,1)} fusion(bf16[1,8,32,1024]{2,1,0,3:T(8,128)(2,1)} %fusion.8, bf16[3,8,32,1024]{2,1,0,3:T(8,128)(2,1)S(1)} %bitcast.65), kind=kLoop, calls=%fused_computation.82 | loop fusion | flops 1048576 | bytes 4194304
  44.8 10.6 %reshape.340 = bf16[4,2,131072]{2,1,0:T(2,128)(2,1)} reshape(bf16[1024,4,8,32]{3,2,1,0:T(8,128)(2,1)} %fusion.33) | data formatting | bytes 4194304
  55.4 5.0 %all-to-all-start = ((bf16[4,2,131072]{2,1,0:T(2,128)(2,1)}), bf16[4,2,131072]{2,1,0:T(2,128)(2,1)S(1)}, u32[]{:S(2)}, u32[]{:S(2)}) async-start(bf16[4,2,131072]{2,1,0:T(2,128)(2,1)} %reshape.340), calls=%async_computation | async-start | bytes 4194304 | tf_op jit(solution)/shard_map/all_to_all | solution.py:68
  60.4 0.7 fusion.32
  69.8 0.7 fusion.31
  79.1 29.5 %all-to-all-done = bf16[4,2,131072]{2,1,0:T(2,128)(2,1)S(1)} async-done(((bf16[4,2,131072]{2,1,0:T(2,128)(2,1)}), bf16[4,2,131072]{2,1,0:T(2,128)(2,1)S(1)}, u32[]{:S(2)}, u32[]{:S(2)}) %all-to-all-start) | async-done | bytes 2097184 | tf_op jit(solution)/shard_map/all_to_all | solution.py:68
  108.6 5.6 %reshape.341 = bf16[1024,4,8,32]{3,2,1,0:T(8,128)(2,1)} reshape(bf16[4,2,131072]{2,1,0:T(2,128)(2,1)S(1)} %all-to-all-done) | data formatting | bytes 4194304
  114.3 8.8 %copy.35 = bf16[4,8,32,4,256]{4,1,2,3,0:T(8,128)(2,1)S(1)} copy(bf16[4,8,32,4,256]{2,1,0,4,3:T(8,128)(2,1)} %bitcast.63) | data formatting | bytes 4194304 | tf_op jit(solution)/shard_map/all_to_all | solution.py:68
  123.1 4.5 %dynamic-slice_select_fusion.6 = (bf16[4,16,8192]{2,1,0:T(8,128)(2,1)}, bf16[4,16,8192]{2,1,0:T(8,128)(2,1)}, bf16[4,16,8192]{2,1,0:T(8,128)(2,1)}, bf16[4,16,81...) fusion(bf16[4,32,8192]{2,1,0:T(8,128)(2,1)S(1)} %bitcast.61, ...), kind=kLoop, calls=%fused_computation.35 | loop fusion | flops 3670016 | bytes 14680099 | tf_op jit(solution)/shard_map/jit(_where)/select_n | solution.py:14
  127.7 0.1 iota_subtract_fusion
  127.7 0.1 subtract_select_fusion
  127.9 0.2 multiply_convert_fusion.1
  128.2 0.1 multiply_convert_fusion.3
  128.3 7.6 %convolution_bitcast_fusion = f32[4,98,8192]{2,1,0:T(8,128)} fusion(bf16[4,32,8192]{2,1,0:T(8,128)(2,1)S(1)} %bitcast.62, bf16[98,32]{1,0:T(8,128)(2,1)S(1)} %convert_element_type.85), kind=kOutput, calls=%fused_computation | convolution fusion | flops 205520896 | bytes 14948480 | tf_op jit(solution)/shard_map/rt,qtn->qrn/dot_general | solution.py:70
  135.9 105.2 %all-reduce.3.cloned.1.call-done = (bf16[4,16,8192]{2,1,0:T(8,128)(2,1)}, bf16[4,16,8192]{2,1,0:T(8,128)(2,1)}, bf16[4,16,8192]{2,1,0:T(8,128)(2,1)}, bf16[4,16,...) async-done(((bf16[4,16,8192]{2,1,0:T(8,128)(2,1)}, bf16[4,16,8192]{2,1,0:T(8,128)(2,1)}, ...) | async-done | bytes 7340048 | tf_op jit(solution)/shard_map/psum | solution.py:14
  241.1 1.7 convolution_bitcast_fusion.1
  242.9 0.4 convolution_bitcast_fusion.2
  243.3 0.8 copy-done.6
  244.1 0.4 convolution_bitcast_fusion.3
  244.5 0.1 copy-done.5
  244.6 1.7 convolution_bitcast_fusion.4
  246.3 1.7 convolution_bitcast_fusion.5
  248.1 1.7 convolution_bitcast_fusion.6
  249.8 1.8 convolution_bitcast_fusion.7
  251.6 15.3 %subtract_add_fusion = f32[4,7,8192]{2,1,0:T(8,128)} fusion(f32[4,98,8192]{2,1,0:T(8,128)} %convolution_bitcast_fusion, f32[4,14,8192]{2,1,0:T(8,128)S(1)} %convolution_bitcast_fusion.1, f32[4,14,8192]{2,1,0:T(8,128)S(1)} %convolution_bitcast_fusion.2, f32[4,14,8192]{2,1,0:T(8,128)S(1)} %convolution_bitcast_fusion.3, ...), kind=kLoop, calls=%fused_computation.27 | loop fusion | flops 6193152 | bytes 26607616 | tf_op jit(solution)/shard_map/add | solution.py:90
  266.9 15.6 %add_add_fusion = f32[4,7,8192]{2,1,0:T(8,128)} fusion(f32[4,98,8192]{2,1,0:T(8,128)} %convolution_bitcast_fusion, f32[4,14,8192]{2,1,0:T(8,128)S(1)} %convolution_bitcast_fusion.1, f32[4,14,8192]{2,1,0:T(8,128)S(1)} %convolution_bitcast_fusion.2, f32[4,14,8192]{2,1,0:T(8,128)S(1)} %convolution_bitcast_fusion.3, ...), kind=kLoop, calls=%fused_computation.28 | loop fusion | flops 6193152 | bytes 26607616 | tf_op jit(solution)/shard_map/add | solution.py:89
  282.6 1.8 reshape.339
  284.4 0.5 reshape.338
  284.9 0.2 copy_multiply_fusion
  285.1 1.3 copy.39
  (37 shorter events, 0.2 us)
Async XLA Ops:
  7.9 9.5 %copy-start = (bf16[3,8,32,1024]{3,2,1,0:T(8,128)(2,1)S(1)}, bf16[3,8,32,1024]{3,2,1,0:T(8,128)(2,1)}, u32[]{:S(2)}) copy-start(bf16[3,8,32,1024]{3,2,1,0:T(8,128)(2,1)} %param.3) | copy-start | bytes 4718596
  8.1 5.3 %collective-permute-start = (bf16[2,8,2,1024]{3,1,2,0:T(8,128)(2,1)S(1)}, bf16[2,8,2,1024]{3,1,2,0:T(8,128)(2,1)S(1)}, u32[]{:S(2)}, u32[]{:S(2)}) collective-permute-start(bf16[2,8,2,1024]{3,1,2,0:T(8,128)(2,1)S(1)} %copy.47), channel_id=1, source_target_pairs={{0,16},{16,0},{1,17},{17,1},{2,18},{18,2},{3,19},{19,3},{4,20},{20... | collective-permute-start | bytes 196616 | tf_op jit(solution)/shard_map/ppermute | solution.py:24
  11.1 4.3 %collective-permute-start.1 = (bf16[2,8,2,1024]{3,1,2,0:T(8,128)(2,1)S(1)}, bf16[2,8,2,1024]{3,1,2,0:T(8,128)(2,1)S(1)}, u32[]{:S(2)}, u32[]{:S(2)}) collective-permute-start(bf16[2,8,2,1024]{3,1,2,0:T(8,128)(2,1)S(1)} %copy.48), channel_id=1, source_target_pairs={{16,0},{0,16},{17,1},{1,17},{18,2},{2,18},{19,3},{3,19},{20,4},{4,... | collective-permute-start | bytes 196616 | tf_op jit(solution)/shard_map/ppermute | solution.py:25
  15.6 7.9 %collective-permute-start.2 = (bf16[2,8,36,2]{3,1,2,0:T(8,128)(2,1)S(1)}, bf16[2,8,36,2]{3,1,2,0:T(8,128)(2,1)S(1)}, u32[]{:S(2)}, u32[]{:S(2)}) collective-permute-start(bf16[2,8,36,2]{3,1,2,0:T(8,128)(2,1)S(1)} %get-tuple-element.22), channel_id=1, source_target_pairs={{0,4},{4,8},{8,12},{12,0},{1,5},{5,9},{9,13},{13,1},{2,6},{6,10},{... | collective-permute-start | bytes 6920 | tf_op jit(solution)/shard_map/ppermute | solution.py:24
  15.7 7.8 %collective-permute-start.3 = (bf16[2,8,36,2]{3,1,2,0:T(8,128)(2,1)S(1)}, bf16[2,8,36,2]{3,1,2,0:T(8,128)(2,1)S(1)}, u32[]{:S(2)}, u32[]{:S(2)}) collective-permute-start(bf16[2,8,36,2]{3,1,2,0:T(8,128)(2,1)S(1)} %get-tuple-element.21), channel_id=1, source_target_pairs={{4,0},{8,4},{12,8},{0,12},{5,1},{9,5},{13,9},{1,13},{6,2},{10,6},{... | collective-permute-start | bytes 6920 | tf_op jit(solution)/shard_map/ppermute | solution.py:25
  32.3 5.7 %slice-start = ((s8[6291456]{0:T(1024)(128)(4,1)}), s8[4194304]{0:T(1024)(128)(4,1)S(1)}, s32[]{:S(2)}) async-start(s8[6291456]{0:T(1024)(128)(4,1)} %bitcast.64), calls=%async_computation.2 | async-start | bytes 8388608
  33.6 4.5 %slice-start.1 = ((s8[6291456]{0:T(1024)(128)(4,1)}), s8[2097152]{0:T(1024)(128)(4,1)S(1)}, s32[]{:S(2)}) async-start(s8[6291456]{0:T(1024)(128)(4,1)} %bitcast.64), calls=%async_computation.3 | async-start | bytes 4194304
  55.4 5.0 %copy-start.8 = (s32[7]{0:T(128)S(1)}, s32[7]{0:T(128)}, u32[]{:S(2)}) copy-start(s32[7]{0:T(128)} %param.4) | copy-start | bytes 88
  55.4 14.4 %copy-start.9 = (s32[7]{0:T(128)S(1)}, s32[7]{0:T(128)}, u32[]{:S(2)}) copy-start(s32[7]{0:T(128)} %param.5) | copy-start | bytes 88
  55.4 53.3 %all-to-all-start = ((bf16[4,2,131072]{2,1,0:T(2,128)(2,1)}), bf16[4,2,131072]{2,1,0:T(2,128)(2,1)S(1)}, u32[]{:S(2)}, u32[]{:S(2)}) async-start(bf16[4,2,131072]{2,1,0:T(2,128)(2,1)} %reshape.340), calls=%async_computation | async-start | bytes 4194304 | tf_op jit(solution)/shard_map/all_to_all | solution.py:68
  60.4 180.7 %all-reduce.3.cloned.1.call-start = ((), (), s32[]{:S(2)}) async-start(), calls=%async_computation.1 | async-start | bytes 14680064 | tf_op jit(solution)/shard_map/psum | solution.py:14
  241.1 1.7 copy-start.7
  242.9 1.2 copy-start.6
  243.3 1.3 copy-start.5
  244.5 1.8 copy-start.4
  246.3 1.8 copy-start.3
  248.1 1.7 copy-start.2
  282.6 1.8 copy-start.1
Sparse Core Ops, SparseCore 0:
  127.8 113.3 all-reduce.2
where the time goes:
time: 294 us; the launch traced here: 293 us
  waiting for transfers between devices  138 us (47%)
  other arithmetic  50.1 us (17%)
  local copies, waits for them, and re-layouts  46.7 us (16%)
  between operations  31 us (11%)
  matrix products  17.1 us (6%)
  starting transfers between devices  9.91 us (3%)
    psum x1, waiting for transfers between devices, from_root(): return lax.psum(jnp.where(mine, shard, jnp.zeros_like(shard)), axis)  105 us
    all_to_all x1, waiting for transfers between devices, shards(): lax.all_to_all(fields, 'ta', split_axis=3, concat_axis=1, tiled=True)  29.5 us
    unnamed x31, local copies, waits for them, and re-layouts  23.8 us
    add x1, other arithmetic, shards(): cospectrum + (remote_cos * cosine_part_here + remote_sin * local_sin)  15.6 us
    add x1, other arithmetic, shards(): quadrature_spectrum + (remote_cos * local_sin - remote_sin * cosine_part_...  15.3 us
    dot_general x7, matrix products, shards(): jnp.einsum('rt,qtn->qrn', window_rows, arrived, preferred_element_type=jn...  9.5 us
    all_to_all x1, local copies, waits for them, and re-layouts, shards(): lax.all_to_all(fields, 'ta', split_axis=3, concat_axis=1, tiled=True)  8.82 us
    dot_general x1, matrix products, shards(): jnp.einsum('rt,qtn->qrn', segment_rows, flat_series, preferred_element_ty...  7.59 us
  transfers between devices with their start and end apart: 6, of which 4 were waited for; matrix products, arithmetic and copies ran while one was open for 6% of the time, Pallas kernels for 0%

commit v1 on v0

--- a/solution.py
+++ b/solution.py
@@ -7,6 +7,18 @@
 SEG = 16
 NSEG = 7
 F = 7
+
+
+def sent_to_each(x, axis, split, join):
+    ways, here = (lax.axis_size(axis), lax.axis_index(axis))
+    width = x.shape[split] // ways
+    turned = jnp.roll(x, -here * width, axis=split)
+    got = [lax.slice_in_dim(turned, 0, width, axis=split)]
+    for far in range(1, ways):
+        sent = lax.slice_in_dim(turned, far * width, (far + 1) * width, axis=split)
+        got.append(lax.ppermute(sent, axis, [(d, (d + far) % ways) for d in range(ways)]))
+    line = jnp.concatenate(got[::-1], axis=join)
+    return jnp.roll(line, (here + 1) * got[0].shape[join], axis=join)
 
 
 def from_root(shard, axis, root):
@@ -65,7 +77,7 @@
     fields = jnp.concatenate([velocity, vorticity[None]], axis=0)
     step_count_total = velocity.shape[1] * lax.axis_size("ta")
     segment_rows = dft_table(offsets, step_count_total)
-    series = lax.all_to_all(fields, "ta", split_axis=3, concat_axis=1, tiled=True)
+    series = sent_to_each(fields, "ta", 3, 1)
     flat_series = series.reshape(series.shape[0], series.shape[1], -1)
     power_spectra = jnp.einsum(
         "rt,qtn->qrn", segment_rows, flat_series, preferred_element_type=jnp.float32

time: 294 us -> 257 us (0.87)
  local copies, waits for them, and re-layouts: 46.7 us -> 17.8 us
  other arithmetic: 50.1 us -> 39.3 us
  waiting for transfers between devices: 138 us -> 142 us
    all_to_all x1 -> x0, waiting for transfers between devices: 29.5 us -> none  [shards(): lax.all_to_all(fields, 'ta', split_axis=3, concat_axis=1, tiled=True)]
    ppermute x0 -> x3, waiting for transfers between devices: none -> 26.5 us  [sent_to_each(): lax.ppermute(sent, axis, [(d, (d + far) % ways) for d in range(ways)])]
    unnamed x31 -> x27, local copies, waits for them, and re-layouts: 23.8 us -> 3.79 us
    all_to_all x1 -> x0, local copies, waits for them, and re-layouts: 8.82 us -> none  [shards(): lax.all_to_all(fields, 'ta', split_axis=3, concat_axis=1, tiled=True)]
    unnamed x2 -> x0, other arithmetic: 6.74 us -> none
    all_to_all x1 -> x0, starting transfers between devices: 5 us -> none  [shards(): lax.all_to_all(fields, 'ta', split_axis=3, concat_axis=1, tiled=True)]
    concatenate x3 -> x1, local copies, waits for them, and re-layouts: 6.07 us -> 1.46 us  [padded_2(): shard = jnp.concatenate([before, shard, after], axis=dim)]
    ppermute x0 -> x3, starting transfers between devices: none -> 4.58 us  [sent_to_each(): lax.ppermute(sent, axis, [(d, (d + far) % ways) for d in range(ways)])]
  transfers between devices with their start and end apart: 6 -> 8, of which waited for: 4 -> 6; matrix products, arithmetic and copies ran while one was open for 6% -> 4% of each run, Pallas kernels for 0% -> 0%
where the time goes in v1:
time: 257 us
  waiting for transfers between devices  142 us (55%)
  other arithmetic  39.3 us (15%)
  between operations  30.8 us (12%)
  local copies, waits for them, and re-layouts  17.8 us (7%)
  matrix products  17.3 us (7%)
  starting transfers between devices  9.48 us (4%)
    psum x1, waiting for transfers between devices, from_root(): return lax.psum(jnp.where(mine, shard, jnp.zeros_like(shard)), axis)  107 us
    ppermute x3, waiting for transfers between devices, sent_to_each(): lax.ppermute(sent, axis, [(d, (d + far) % ways) for d in range(ways)])  26.5 us
    add x1, other arithmetic, shards(): cospectrum + (remote_cos * cosine_part_here + remote_sin * local_sin)  15.5 us
    add x1, other arithmetic, shards(): quadrature_spectrum + (remote_cos * local_sin - remote_sin * cosine_part_...  15.3 us
    dot_general x7, matrix products, shards(): jnp.einsum('rt,qtn->qrn', window_rows, arrived, preferred_element_type=jn...  9.52 us
    dot_general x1, matrix products, shards(): jnp.einsum('rt,qtn->qrn', segment_rows, flat_series, preferred_element_ty...  7.8 us
  transfers between devices with their start and end apart: 8, of which 6 were waited for; matrix products, arithmetic and copies ran while one was open for 4% of the time, Pallas kernels for 0%

profile of v1, /device:TPU:0, one launch (start us, length us, event | category | flops | bytes accessed | tf_op | source)
XLA Modules:
  0.0 256.6 jit_solution(5635522639874455729)
XLA Ops:
  6.5 1.3 fusion.32
  7.8 0.1 pad_maximum_fusion.3
  7.9 3.0 %collective-permute-start.1 = (bf16[2,8,2,1024]{3,2,1,0:T(2,128)(2,1)S(1)}, bf16[2,8,2,1024]{3,2,1,0:T(2,128)(2,1)S(1)}, u32[]{:S(2)}, u32[]{:S(2)}) collective-permute-start(bf16[2,8,2,1024]{3,2,1,0:T(2,128)(2,1)S(1)} %get-tuple-element.27), channel_id=1, source_target_pairs={{16,0},{0,16},{17,1},{1,17},{18,2},{2,18},{19,3},{3,19},{20,4},{4,... | collective-permute-start | bytes 196616 | tf_op jit(solution)/shard_map/ppermute | solution.py:37
  11.1 2.3 collective-permute-done.1
  13.3 1.9 collective-permute-done
  15.2 0.7 pad_maximum_fusion.1
  16.0 0.1 fusion.33
  16.2 1.7 collective-permute-start.3
  17.9 3.0 %collective-permute-done.2 = bf16[2,8,36,2]{3,2,1,0:T(8,128)(2,1)S(1)} collective-permute-done((bf16[2,8,36,2]{3,2,1,0:T(8,128)(2,1)S(1)}, bf16[2,8,36,2]{3,2,1,0:T(8,128)(2,1)S(1)}, u32[]{:S(2)}, u32[]{:S(2)}) %collective-permute-start.2) | collective-permute-done | bytes 2336 | tf_op jit(solution)/shard_map/ppermute | solution.py:36
  20.9 0.8 collective-permute-done.3
  21.7 1.5 concatenate.21
  23.2 0.2 convert_element_type.78
  23.4 0.4 slice_bitcast_fusion
  23.8 0.1 slice_bitcast_fusion.1
  23.9 0.9 fusion.11
  24.8 0.5 copy-done
  25.3 1.2 fusion.1
  26.5 1.2 fusion.31
  27.7 3.6 %collective-permute-start.4 = (bf16[4,8,32,256]{3,2,1,0:T(8,128)(2,1)}, bf16[4,8,32,256]{3,2,1,0:T(8,128)(2,1)S(1)}, u32[]{:S(2)}, u32[]{:S(2)}) collective-permute-start(bf16[4,8,32,256]{3,2,1,0:T(8,128)(2,1)} %get-tuple-element.21), channel_id=1, source_target_pairs={{0,3},{1,0},{2,1},{3,2},{4,7},{5,4},{6,5},{7,6},{8,11},{9,8},{10,9... | collective-permute-start | bytes 1572872 | tf_op jit(solution)/shard_map/ppermute | solution.py:19
  31.3 1.0 collective-permute-start.6
  32.3 0.6 fusion.35
  41.4 0.7 fusion.34
  50.8 26.5 %collective-permute-done.5 = bf16[4,8,32,256]{3,2,1,0:T(8,128)(2,1)S(1)} collective-permute-done((bf16[4,8,32,256]{3,2,1,0:T(8,128)(2,1)}, bf16[4,8,32,256]{3,2,1,0:T(8,128)(2,1)S(1)}, u32[]{:S(2)}, u32[]{:S(2)}) %collective-permute-start.5) | collective-permute-done | bytes 524320 | tf_op jit(solution)/shard_map/ppermute | solution.py:19
  77.3 1.1 constant_dynamic-update-slice_fusion.3
  78.6 1.1 constant_dynamic-update-slice_fusion
  79.8 1.5 constant_dynamic-slice_fusion
  81.3 2.9 %reshape.333 = bf16[4,32,8192]{2,1,0:T(8,128)(2,1)S(1)} reshape(bf16[4,32,32,256]{3,2,1,0:T(8,128)(2,1)} %constant_dynamic-slice_fusion) | data formatting | bytes 4194304 | tf_op jit(solution)/shard_map/reshape | solution.py:81
  84.2 4.5 %dynamic-slice_select_fusion.6 = (bf16[4,16,8192]{2,1,0:T(8,128)(2,1)}, bf16[4,16,8192]{2,1,0:T(8,128)(2,1)}, bf16[4,16,8192]{2,1,0:T(8,128)(2,1)}, bf16[4,16,81...) fusion(bf16[4,32,8192]{2,1,0:T(8,128)(2,1)S(1)} %reshape.333, ...), kind=kLoop, calls=%fused_computation.40 | loop fusion | flops 3670016 | bytes 14680099 | tf_op jit(solution)/shard_map/jit(_where)/select_n | solution.py:26
  88.8 0.1 subtract_select_fusion
  88.9 0.2 multiply_convert_fusion.1
  89.2 0.1 multiply_convert_fusion.3
  89.4 7.8 %convolution_bitcast_fusion = f32[4,98,8192]{2,1,0:T(8,128)} fusion(bf16[4,32,8192]{2,1,0:T(8,128)(2,1)S(1)} %reshape.333, bf16[98,32]{1,0:T(8,128)(2,1)S(1)} %convert_element_type.85), kind=kOutput, calls=%fused_computation | convolution fusion | flops 205520896 | bytes 14948480 | tf_op jit(solution)/shard_map/rt,qtn->qrn/dot_general | solution.py:82
  97.2 107.4 %all-reduce.3.cloned.1.call-done = (bf16[4,16,8192]{2,1,0:T(8,128)(2,1)}, bf16[4,16,8192]{2,1,0:T(8,128)(2,1)}, bf16[4,16,8192]{2,1,0:T(8,128)(2,1)}, bf16[4,16,...) async-done(((bf16[4,16,8192]{2,1,0:T(8,128)(2,1)}, bf16[4,16,8192]{2,1,0:T(8,128)(2,1)}, ...) | async-done | bytes 7340048 | tf_op jit(solution)/shard_map/psum | solution.py:26
  204.6 1.7 convolution_bitcast_fusion.1
  206.3 0.4 convolution_bitcast_fusion.2
  206.8 0.8 copy-done.6
  207.5 0.4 convolution_bitcast_fusion.3
  208.0 0.1 copy-done.5
  208.1 1.8 convolution_bitcast_fusion.4
  209.8 1.7 convolution_bitcast_fusion.5
  211.6 1.7 convolution_bitcast_fusion.6
  213.3 1.8 convolution_bitcast_fusion.7
  215.0 15.3 %subtract_add_fusion = f32[4,7,8192]{2,1,0:T(8,128)} fusion(f32[4,98,8192]{2,1,0:T(8,128)} %convolution_bitcast_fusion, f32[4,14,8192]{2,1,0:T(8,128)S(1)} %convolution_bitcast_fusion.1, f32[4,14,8192]{2,1,0:T(8,128)S(1)} %convolution_bitcast_fusion.2, f32[4,14,8192]{2,1,0:T(8,128)S(1)} %convolution_bitcast_fusion.3, ...), kind=kLoop, calls=%fused_computation.32 | loop fusion | flops 6193152 | bytes 26607616 | tf_op jit(solution)/shard_map/add | solution.py:102
  230.4 15.5 %add_add_fusion = f32[4,7,8192]{2,1,0:T(8,128)} fusion(f32[4,98,8192]{2,1,0:T(8,128)} %convolution_bitcast_fusion, f32[4,14,8192]{2,1,0:T(8,128)S(1)} %convolution_bitcast_fusion.1, f32[4,14,8192]{2,1,0:T(8,128)S(1)} %convolution_bitcast_fusion.2, f32[4,14,8192]{2,1,0:T(8,128)S(1)} %convolution_bitcast_fusion.3, ...), kind=kLoop, calls=%fused_computation.33 | loop fusion | flops 6193152 | bytes 26607616 | tf_op jit(solution)/shard_map/add | solution.py:101
  245.9 1.8 reshape.338
  247.7 0.5 reshape.337
  248.2 0.2 copy_multiply_fusion
  248.4 1.3 copy.9
  (37 shorter events, 0.7 us)
Async XLA Ops:
  6.5 198.0 %all-reduce.3.cloned.1.call-start = ((), (), s32[]{:S(2)}) async-start(), calls=%async_computation | async-start | bytes 14680064 | tf_op jit(solution)/shard_map/psum | solution.py:26
  7.9 5.4 %collective-permute-start.1 = (bf16[2,8,2,1024]{3,2,1,0:T(2,128)(2,1)S(1)}, bf16[2,8,2,1024]{3,2,1,0:T(2,128)(2,1)S(1)}, u32[]{:S(2)}, u32[]{:S(2)}) collective-permute-start(bf16[2,8,2,1024]{3,2,1,0:T(2,128)(2,1)S(1)} %get-tuple-element.27), channel_id=1, source_target_pairs={{16,0},{0,16},{17,1},{1,17},{18,2},{2,18},{19,3},{3,19},{20,4},{4,... | collective-permute-start | bytes 196616 | tf_op jit(solution)/shard_map/ppermute | solution.py:37
  11.0 4.3 %collective-permute-start = (bf16[2,8,2,1024]{3,2,1,0:T(2,128)(2,1)S(1)}, bf16[2,8,2,1024]{3,2,1,0:T(2,128)(2,1)S(1)}, u32[]{:S(2)}, u32[]{:S(2)}) collective-permute-start(bf16[2,8,2,1024]{3,2,1,0:T(2,128)(2,1)S(1)} %get-tuple-element.26), channel_id=1, source_target_pairs={{0,16},{16,0},{1,17},{17,1},{2,18},{18,2},{3,19},{19,3},{4,20},{20... | collective-permute-start | bytes 196616 | tf_op jit(solution)/shard_map/ppermute | solution.py:36
  16.1 4.8 %collective-permute-start.2 = (bf16[2,8,36,2]{3,2,1,0:T(8,128)(2,1)S(1)}, bf16[2,8,36,2]{3,2,1,0:T(8,128)(2,1)S(1)}, u32[]{:S(2)}, u32[]{:S(2)}) collective-permute-start(bf16[2,8,36,2]{3,2,1,0:T(8,128)(2,1)S(1)} %get-tuple-element.25), channel_id=1, source_target_pairs={{0,4},{4,8},{8,12},{12,0},{1,5},{5,9},{9,13},{13,1},{2,6},{6,10},{... | collective-permute-start | bytes 6920 | tf_op jit(solution)/shard_map/ppermute | solution.py:36
  16.2 5.5 %collective-permute-start.3 = (bf16[2,8,36,2]{3,2,1,0:T(8,128)(2,1)S(1)}, bf16[2,8,36,2]{3,2,1,0:T(8,128)(2,1)S(1)}, u32[]{:S(2)}, u32[]{:S(2)}) collective-permute-start(bf16[2,8,36,2]{3,2,1,0:T(8,128)(2,1)S(1)} %get-tuple-element.24), channel_id=1, source_target_pairs={{4,0},{8,4},{12,8},{0,12},{5,1},{9,5},{13,9},{1,13},{6,2},{10,6},{... | collective-permute-start | bytes 6920 | tf_op jit(solution)/shard_map/ppermute | solution.py:37
  23.9 1.4 copy-start
  26.5 5.8 %copy-start.8 = (s32[7]{0:T(128)S(1)}, s32[7]{0:T(128)}, u32[]{:S(2)}) copy-start(s32[7]{0:T(128)} %param.4) | copy-start | bytes 88
  26.5 14.9 %copy-start.9 = (s32[7]{0:T(128)S(1)}, s32[7]{0:T(128)}, u32[]{:S(2)}) copy-start(s32[7]{0:T(128)} %param.5) | copy-start | bytes 88
  27.7 23.0 %collective-permute-start.4 = (bf16[4,8,32,256]{3,2,1,0:T(8,128)(2,1)}, bf16[4,8,32,256]{3,2,1,0:T(8,128)(2,1)S(1)}, u32[]{:S(2)}, u32[]{:S(2)}) collective-permute-start(bf16[4,8,32,256]{3,2,1,0:T(8,128)(2,1)} %get-tuple-element.21), channel_id=1, source_target_pairs={{0,3},{1,0},{2,1},{3,2},{4,7},{5,4},{6,5},{7,6},{8,11},{9,8},{10,9... | collective-permute-start | bytes 1572872 | tf_op jit(solution)/shard_map/ppermute | solution.py:19
  31.3 46.0 %collective-permute-start.5 = (bf16[4,8,32,256]{3,2,1,0:T(8,128)(2,1)}, bf16[4,8,32,256]{3,2,1,0:T(8,128)(2,1)S(1)}, u32[]{:S(2)}, u32[]{:S(2)}) collective-permute-start(bf16[4,8,32,256]{3,2,1,0:T(8,128)(2,1)} %get-tuple-element.20), channel_id=1, source_target_pairs={{0,2},{1,3},{2,0},{3,1},{4,6},{5,7},{6,4},{7,5},{8,10},{9,11},{10,... | collective-permute-start | bytes 1572872 | tf_op jit(solution)/shard_map/ppermute | solution.py:19
  31.3 46.0 %collective-permute-start.6 = (bf16[4,8,32,256]{3,2,1,0:T(8,128)(2,1)}, bf16[4,8,32,256]{3,2,1,0:T(8,128)(2,1)}, u32[]{:S(2)}, u32[]{:S(2)}) collective-permute-start(bf16[4,8,32,256]{3,2,1,0:T(8,128)(2,1)} %get-tuple-element.19), channel_id=1, source_target_pairs={{0,1},{1,2},{2,3},{3,0},{4,5},{5,6},{6,7},{7,4},{8,9},{9,10},{10,1... | collective-permute-start | bytes 1572872 | tf_op jit(solution)/shard_map/ppermute | solution.py:19
  204.6 1.7 copy-start.7
  206.3 1.2 copy-start.6
  206.7 1.3 copy-start.5
  208.0 1.9 copy-start.4
  209.8 1.7 copy-start.3
  211.6 1.7 copy-start.2
  245.9 1.8 copy-start.1
Sparse Core Ops, SparseCore 0:
  88.8 115.6 all-reduce.2
